TPU v7x, 512 devices: a whole 4x4x16 slice. The times are simulated.
512 devices in a mesh: tx: 8 (over x, core), ty: 16 (over z), tz: 4 (over y).
Axes of the slice: x: 4, y: 4, z: 16, core: 2. Of those that a mesh axis runs over, the one named last changes fastest.
Arguments:
- start_block: float32 [64, 1048576], P(None, ('tx', 'ty', 'tz'))
- weights: bfloat16 [8192, 6, 128, 128], P(('tx', 'ty', 'tz')), may hold values from 0 to 0.25, as said below
- neighbours: int32 [8192, 6], P(('tx', 'ty', 'tz')), may hold values from 0 to 123, as said below
- boundary: int32 [2048], P(('tx', 'ty', 'tz')), may hold values from 0 to 15, as said below
Outputs:
- basis: float32 [64, 1048576], P(None, ('tx', 'ty', 'tz'))
- rfactor: float32 [64, 64], replicated
Inputs may be any that keep to these rules, and one draw needn't show every extreme that they name: `neighbours`: slot 0 of block row b is b % 16; in the last of each device's 16 rows slot 1 is 123. `boundary`: each device's 4 entries are distinct, the last of them 16 - 1. For each block row b and point p, exactly 16 of the entries weights[b, s, q, p] over all slots s and rows q are nonzero, each positive.
All inputs are finite; a program needn't handle non-finite values.
Results may differ from a plain program's by a relative error of at most 0.00075.
Values may be sent and summed in bfloat16 or wider, within the bound.
No kernel may reach another device: no remote copies, remote signals or barrier semaphores. Data moves between devices by JAX's collectives and lax.ppermute only.
A program may use at most 64 MiB of HBM per device.

v0:
```python
import jax
import jax.numpy as jnp
from jax import lax
from jax.sharding import PartitionSpec as P


def extended(block, sides, width):
    for axis, dim in sides:
        count = lax.axis_size(axis)
        forward = [(i, i + 1) for i in range(count - 1)]
        backward = [(target, source) for source, target in forward]
        low = lax.ppermute(
            lax.slice_in_dim(block, block.shape[dim] - width, None, axis=dim), axis, forward
        )
        high = lax.ppermute(lax.slice_in_dim(block, 0, width, axis=dim), axis, backward)
        block = jnp.concatenate([low, block, high], axis=dim)
    return block


def take_edges(grid, boundary):
    return jnp.take(grid, boundary, axis=1)[:, None, None, None]


def boundary_halo(edge_part):
    return extended(edge_part, (("tx", 1), ("ty", 2), ("tz", 3)), 1)


def as_pool(haloed):
    return haloed.reshape(haloed.shape[0], -1, haloed.shape[-1])


def apply_operator(current, own_grid, far_grid, degree, weights, neighbours):
    pool_grid = jnp.concatenate([own_grid, far_grid], axis=1)
    picked = jnp.take(pool_grid, neighbours, axis=1)
    product = jnp.einsum("kisq,isqp->kip", picked, weights, preferred_element_type=jnp.float32)
    return current * (1.0 - degree * 0.125) + product.reshape(current.shape) * 0.125


def lower_factor(mixed):
    local_gram = jnp.dot(
        mixed, mixed.T, precision=lax.Precision.HIGHEST, preferred_element_type=jnp.float32
    )
    total = lax.psum(local_gram, ("tx", "ty", "tz"))
    return jnp.linalg.cholesky(total)


def solve_lower(lower, values):
    return lax.linalg.triangular_solve(lower, values, left_side=True, lower=True)


def per_device(start_block, weights, neighbours, boundary):
    width, points = start_block.shape
    block_size = weights.shape[-1]
    blocks = points // block_size
    devices = lax.axis_size("tx") * lax.axis_size("ty") * lax.axis_size("tz")
    root_scale = float(points * devices) ** 0.5
    degree = jnp.sum(weights, axis=(1, 2), dtype=jnp.float32).reshape(points)
    own_grid = start_block.astype(jnp.bfloat16).reshape(width, blocks, block_size)
    far_grid = as_pool(boundary_halo(take_edges(own_grid, boundary)))
    mixed = apply_operator(start_block, own_grid, far_grid, degree, weights, neighbours)
    lower = lower_factor(mixed)
    current = solve_lower(lower, mixed) * root_scale
    own_grid = current.astype(jnp.bfloat16).reshape(width, blocks, block_size)
    far_grid = as_pool(boundary_halo(take_edges(own_grid, boundary)))
    mixed = apply_operator(current, own_grid, far_grid, degree, weights, neighbours)
    lower = lower_factor(mixed)
    basis = solve_lower(lower, mixed) * root_scale
    return (basis, lower.T / root_scale)


def solution(mesh):
    placed = (
        P(None, ("tx", "ty", "tz")),
        P(("tx", "ty", "tz"), None, None, None),
        P(("tx", "ty", "tz"), None),
        P(("tx", "ty", "tz")),
    )
    return jax.shard_map(
        per_device,
        mesh=mesh,
        in_specs=placed,
        out_specs=(P(None, ("tx", "ty", "tz")), P()),
        check_vma=False,
    )
```

profile of v0, /device:TPU:1, one launch (start us, length us, event | category | flops | bytes accessed | tf_op | source)
XLA Modules:
  0.0 328.7 jit_solution(997474695390738293)
XLA Ops:
  0.6 0.7 compare_and_fusion.1
  1.3 0.7 compare_select_fusion.1
  2.0 1.1 copy_bitcast_fusion.1
  3.1 0.6 gather_fusion
  3.7 8.8 %collective-permute-start.1 = (bf16[64,1,1,1,4,128]{5,0,4,3,2,1:T(8,128)(2,1)S(1)}, bf16[64,1,1,1,4,128]{5,0,4,3,2,1:T(8,128)(2,1)S(1)}, u32[]{:S(2)}, u32[]{:S(2)}) collective-permute-start(bf16[64,1,1,1,4,128]{5,0,4,3,2,1:T(8,128)(2,1)S(1)} %select_bitcast_fusion.1), channel_id=1, source_target_pairs={{64,0},{128,64},{192,128},{256,192},{320,256},{384,320},{448,384},... | collective-permute-start | bytes 196616 | tf_op jit(solution)/shard_map/ppermute | solution.py:15
  12.5 1.9 collective-permute-start
  14.4 0.7 compare_and_fusion
  15.8 1.3 collective-permute-start.3
  17.1 4.0 %collective-permute-start.2 = (bf16[64,3,1,1,4,128]{5,0,4,3,2,1:T(8,128)(2,1)S(1)}, bf16[64,3,1,1,4,128]{5,0,4,3,2,1:T(8,128)(2,1)S(1)}, u32[]{:S(2)}, u32[]{:S(2)}) collective-permute-start(bf16[64,3,1,1,4,128]{5,0,4,3,2,1:T(8,128)(2,1)S(1)} %pad_maximum_fusion.6), channel_id=1, source_target_pairs={{0,4},{4,8},{8,12},{12,16},{16,20},{20,24},{24,28},{28,32},{32,36}... | collective-permute-start | bytes 589832 | tf_op jit(solution)/shard_map/ppermute | solution.py:12
  21.1 0.7 compare_select_fusion
  21.9 2.2 collective-permute-done.3
  24.1 0.9 collective-permute-done.2
  25.0 1.3 collective-permute-start.5
  26.3 4.0 %collective-permute-start.4 = (bf16[64,3,3,1,4,128]{5,0,4,3,2,1:T(8,128)(2,1)S(1)}, bf16[64,3,3,1,4,128]{5,0,4,3,2,1:T(8,128)(2,1)S(1)}, u32[]{:S(2)}, u32[]{:S(2)}) collective-permute-start(bf16[64,3,3,1,4,128]{5,0,4,3,2,1:T(8,128)(2,1)S(1)} %pad_maximum_fusion.4), channel_id=1, source_target_pairs={{0,1},{1,2},{2,3},{4,5},{5,6},{6,7},{8,9},{9,10},{10,11},{12,13},{... | collective-permute-start | bytes 1769480 | tf_op jit(solution)/shard_map/ppermute | solution.py:12
  30.4 2.4 convert_reduce_fusion
  32.8 7.8 %collective-permute-done.5 = bf16[64,3,3,1,4,128]{5,0,4,3,2,1:T(8,128)(2,1)S(1)} collective-permute-done((bf16[64,3,3,1,4,128]{5,0,4,3,2,1:T(8,128)(2,1)S(1)}, bf16[64,3,3,1,4,128]{5,0,4,3,2,1:T(8,128)(2,1)S(1)}, u32[]{:S(2)}, u32[]{:S(2)}) %collective-permute-start.5) | collective-permute-done | bytes 589856 | tf_op jit(solution)/shard_map/ppermute | solution.py:15
  40.6 0.9 collective-permute-done.4
  41.9 2.0 gather_fusion.1
  43.9 3.2 fusion.23
  47.0 0.6 fusion.30
  47.6 108.8 %psum.14 = f32[64,64]{0,1:T(8,128)S(1)} all-reduce(f32[64,64]{0,1:T(8,128)S(1)} %fusion.30), channel_id=1, replica_groups=mesh['tx'=8,'ty'=16,'tz'=4] {'tx','ty','tz'}, use_global_device_ids=true, to_apply=%region_1.4 | all-reduce | flops 4096 | bytes 32768 | tf_op jit(solution)/shard_map/psum | solution.py:43
  156.5 5.8 %cholesky.44 = f32[64,64]{1,0:T(8,128)S(1)} custom-call(f32[64,64]{1,0:T(8,128)S(1)} %fusion.36), custom_call_target="Cholesky" | custom-call | tf_op jit(solution)/shard_map/jit(cholesky)/cholesky | solution.py:44
  162.4 0.6 compare_reduce_fusion.1
  163.1 0.7 fusion.32
  163.7 4.9 %custom-call.6 = f32[1,64,64]{1,2,0:T(8,128)S(1)} custom-call(f32[1,64,64]{2,1,0:T(8,128)S(1)} %fusion.32), custom_call_target="InvertDiagBlocksLowerTriangular" | custom-call | tf_op jit(solution)/shard_map/triangular_solve/custom-call.0 | solution.py:48
  168.6 0.6 fusion.29
  169.3 0.6 gather_fusion.2
  170.0 2.6 collective-permute-start.7
  172.6 3.0 collective-permute-start.6
  175.6 1.3 collective-permute-done.6
  176.9 1.3 collective-permute-start.9
  178.2 4.3 %collective-permute-start.8 = (bf16[64,3,1,1,4,128]{5,0,4,3,2,1:T(8,128)(2,1)S(1)}, bf16[64,3,1,1,4,128]{5,0,4,3,2,1:T(8,128)(2,1)S(1)}, u32[]{:S(2)}, u32[]{:S(2)}) collective-permute-start(bf16[64,3,1,1,4,128]{5,0,4,3,2,1:T(8,128)(2,1)S(1)} %pad_maximum_fusion.7), channel_id=1, source_target_pairs={{0,4},{4,8},{8,12},{12,16},{16,20},{20,24},{24,28},{28,32},{32,36}... | collective-permute-start | bytes 589832 | tf_op jit(solution)/shard_map/ppermute | solution.py:12
  182.4 2.4 collective-permute-done.9
  184.9 1.8 collective-permute-done.8
  186.7 1.3 collective-permute-start.11
  188.0 4.0 %collective-permute-start.10 = (bf16[64,3,3,1,4,128]{5,0,4,3,2,1:T(8,128)(2,1)S(1)}, bf16[64,3,3,1,4,128]{5,0,4,3,2,1:T(8,128)(2,1)S(1)}, u32[]{:S(2)}, u32[]{:S(2)}) collective-permute-start(bf16[64,3,3,1,4,128]{5,0,4,3,2,1:T(8,128)(2,1)S(1)} %pad_maximum_fusion.5), channel_id=1, source_target_pairs={{0,1},{1,2},{2,3},{4,5},{5,6},{6,7},{8,9},{9,10},{10,11},{12,13},{... | collective-permute-start | bytes 1769480 | tf_op jit(solution)/shard_map/ppermute | solution.py:12
  192.0 11.6 %collective-permute-done.11 = bf16[64,3,3,1,4,128]{5,0,4,3,2,1:T(8,128)(2,1)S(1)} collective-permute-done((bf16[64,3,3,1,4,128]{5,0,4,3,2,1:T(8,128)(2,1)S(1)}, bf16[64,3,3,1,4,128]{5,0,4,3,2,1:T(8,128)(2,1)S(1)}, u32[]{:S(2)}, u32[]{:S(2)}) %collective-permute-start.11) | collective-permute-done | bytes 589856 | tf_op jit(solution)/shard_map/ppermute | solution.py:15
  203.6 0.9 collective-permute-done.10
  204.9 2.0 gather_fusion.3
  206.9 3.1 fusion.17
  210.0 0.6 fusion.31
  210.5 103.8 %psum.15 = f32[64,64]{0,1:T(8,128)S(1)} all-reduce(f32[64,64]{0,1:T(8,128)S(1)} %fusion.31), channel_id=1, replica_groups=mesh['tx'=8,'ty'=16,'tz'=4] {'tx','ty','tz'}, use_global_device_ids=true, to_apply=%region_4.9 | all-reduce | flops 4096 | bytes 32768 | tf_op jit(solution)/shard_map/psum | solution.py:43
  314.5 5.8 %cholesky.55 = f32[64,64]{1,0:T(8,128)S(1)} custom-call(f32[64,64]{1,0:T(8,128)S(1)} %fusion.34), custom_call_target="Cholesky" | custom-call | tf_op jit(solution)/shard_map/jit(cholesky)/cholesky | solution.py:44
  320.4 0.6 compare_reduce_fusion
  321.0 0.7 multiply_bitcast_fusion
  321.7 0.7 copy.42
  322.4 4.9 %custom-call.7 = f32[1,64,64]{1,2,0:T(8,128)S(1)} custom-call(f32[1,64,64]{2,1,0:T(8,128)S(1)} %get-tuple-element.13), custom_call_target="InvertDiagBlocksLowerTriangular" | custom-call | tf_op jit(solution)/shard_map/triangular_solve/custom-call.0 | solution.py:48
  327.3 1.4 convolution_multiply_fusion
  (29 shorter events, 2.3 us)
Async XLA Ops:
  3.7 11.5 %collective-permute-start.1 = (bf16[64,1,1,1,4,128]{5,0,4,3,2,1:T(8,128)(2,1)S(1)}, bf16[64,1,1,1,4,128]{5,0,4,3,2,1:T(8,128)(2,1)S(1)}, u32[]{:S(2)}, u32[]{:S(2)}) collective-permute-start(bf16[64,1,1,1,4,128]{5,0,4,3,2,1:T(8,128)(2,1)S(1)} %select_bitcast_fusion.1), channel_id=1, source_target_pairs={{64,0},{128,64},{192,128},{256,192},{320,256},{384,320},{448,384},... | collective-permute-start | bytes 196616 | tf_op jit(solution)/shard_map/ppermute | solution.py:15
  12.5 3.2 collective-permute-start
  15.8 8.3 %collective-permute-start.3 = (bf16[64,3,1,1,4,128]{5,0,4,3,2,1:T(8,128)(2,1)S(1)}, bf16[64,3,1,1,4,128]{5,0,4,3,2,1:T(8,128)(2,1)S(1)}, u32[]{:S(2)}, u32[]{:S(2)}) collective-permute-start(bf16[64,3,1,1,4,128]{5,0,4,3,2,1:T(8,128)(2,1)S(1)} %pad_maximum_fusion.6), channel_id=1, source_target_pairs={{4,0},{8,4},{12,8},{16,12},{20,16},{24,20},{28,24},{32,28},{36,32}... | collective-permute-start | bytes 589832 | tf_op jit(solution)/shard_map/ppermute | solution.py:15
  17.1 7.9 %collective-permute-start.2 = (bf16[64,3,1,1,4,128]{5,0,4,3,2,1:T(8,128)(2,1)S(1)}, bf16[64,3,1,1,4,128]{5,0,4,3,2,1:T(8,128)(2,1)S(1)}, u32[]{:S(2)}, u32[]{:S(2)}) collective-permute-start(bf16[64,3,1,1,4,128]{5,0,4,3,2,1:T(8,128)(2,1)S(1)} %pad_maximum_fusion.6), channel_id=1, source_target_pairs={{0,4},{4,8},{8,12},{12,16},{16,20},{20,24},{24,28},{28,32},{32,36}... | collective-permute-start | bytes 589832 | tf_op jit(solution)/shard_map/ppermute | solution.py:12
  25.0 15.5 %collective-permute-start.5 = (bf16[64,3,3,1,4,128]{5,0,4,3,2,1:T(8,128)(2,1)S(1)}, bf16[64,3,3,1,4,128]{5,0,4,3,2,1:T(8,128)(2,1)S(1)}, u32[]{:S(2)}, u32[]{:S(2)}) collective-permute-start(bf16[64,3,3,1,4,128]{5,0,4,3,2,1:T(8,128)(2,1)S(1)} %pad_maximum_fusion.4), channel_id=1, source_target_pairs={{1,0},{2,1},{3,2},{5,4},{6,5},{7,6},{9,8},{10,9},{11,10},{13,12},{... | collective-permute-start | bytes 1769480 | tf_op jit(solution)/shard_map/ppermute | solution.py:15
  26.3 15.1 %collective-permute-start.4 = (bf16[64,3,3,1,4,128]{5,0,4,3,2,1:T(8,128)(2,1)S(1)}, bf16[64,3,3,1,4,128]{5,0,4,3,2,1:T(8,128)(2,1)S(1)}, u32[]{:S(2)}, u32[]{:S(2)}) collective-permute-start(bf16[64,3,3,1,4,128]{5,0,4,3,2,1:T(8,128)(2,1)S(1)} %pad_maximum_fusion.4), channel_id=1, source_target_pairs={{0,1},{1,2},{2,3},{4,5},{5,6},{6,7},{8,9},{9,10},{10,11},{12,13},{... | collective-permute-start | bytes 1769480 | tf_op jit(solution)/shard_map/ppermute | solution.py:12
  43.9 3.2 copy-start
  170.0 5.6 %collective-permute-start.7 = (bf16[64,1,1,1,4,128]{5,0,4,3,2,1:T(8,128)(2,1)S(1)}, bf16[64,1,1,1,4,128]{5,0,4,3,2,1:T(8,128)(2,1)S(1)}, u32[]{:S(2)}, u32[]{:S(2)}) collective-permute-start(bf16[64,1,1,1,4,128]{5,0,4,3,2,1:T(8,128)(2,1)S(1)} %select_bitcast_fusion), channel_id=1, source_target_pairs={{64,0},{128,64},{192,128},{256,192},{320,256},{384,320},{448,384},... | collective-permute-start | bytes 196616 | tf_op jit(solution)/shard_map/ppermute | solution.py:15
  172.6 4.3 %collective-permute-start.6 = (bf16[64,1,1,1,4,128]{5,0,4,3,2,1:T(8,128)(2,1)S(1)}, bf16[64,1,1,1,4,128]{5,0,4,3,2,1:T(8,128)(2,1)S(1)}, u32[]{:S(2)}, u32[]{:S(2)}) collective-permute-start(bf16[64,1,1,1,4,128]{5,0,4,3,2,1:T(8,128)(2,1)S(1)} %select_bitcast_fusion), channel_id=1, source_target_pairs={{0,64},{64,128},{128,192},{192,256},{256,320},{320,384},{384,448},... | collective-permute-start | bytes 196616 | tf_op jit(solution)/shard_map/ppermute | solution.py:12
  176.9 8.0 %collective-permute-start.9 = (bf16[64,3,1,1,4,128]{5,0,4,3,2,1:T(8,128)(2,1)S(1)}, bf16[64,3,1,1,4,128]{5,0,4,3,2,1:T(8,128)(2,1)S(1)}, u32[]{:S(2)}, u32[]{:S(2)}) collective-permute-start(bf16[64,3,1,1,4,128]{5,0,4,3,2,1:T(8,128)(2,1)S(1)} %pad_maximum_fusion.7), channel_id=1, source_target_pairs={{4,0},{8,4},{12,8},{16,12},{20,16},{24,20},{28,24},{32,28},{36,32}... | collective-permute-start | bytes 589832 | tf_op jit(solution)/shard_map/ppermute | solution.py:15
  178.2 8.4 %collective-permute-start.8 = (bf16[64,3,1,1,4,128]{5,0,4,3,2,1:T(8,128)(2,1)S(1)}, bf16[64,3,1,1,4,128]{5,0,4,3,2,1:T(8,128)(2,1)S(1)}, u32[]{:S(2)}, u32[]{:S(2)}) collective-permute-start(bf16[64,3,1,1,4,128]{5,0,4,3,2,1:T(8,128)(2,1)S(1)} %pad_maximum_fusion.7), channel_id=1, source_target_pairs={{0,4},{4,8},{8,12},{12,16},{16,20},{20,24},{24,28},{28,32},{32,36}... | collective-permute-start | bytes 589832 | tf_op jit(solution)/shard_map/ppermute | solution.py:12
  186.7 16.9 %collective-permute-start.11 = (bf16[64,3,3,1,4,128]{5,0,4,3,2,1:T(8,128)(2,1)S(1)}, bf16[64,3,3,1,4,128]{5,0,4,3,2,1:T(8,128)(2,1)S(1)}, u32[]{:S(2)}, u32[]{:S(2)}) collective-permute-start(bf16[64,3,3,1,4,128]{5,0,4,3,2,1:T(8,128)(2,1)S(1)} %pad_maximum_fusion.5), channel_id=1, source_target_pairs={{1,0},{2,1},{3,2},{5,4},{6,5},{7,6},{9,8},{10,9},{11,10},{13,12},{... | collective-permute-start | bytes 1769480 | tf_op jit(solution)/shard_map/ppermute | solution.py:15
  188.0 16.5 %collective-permute-start.10 = (bf16[64,3,3,1,4,128]{5,0,4,3,2,1:T(8,128)(2,1)S(1)}, bf16[64,3,3,1,4,128]{5,0,4,3,2,1:T(8,128)(2,1)S(1)}, u32[]{:S(2)}, u32[]{:S(2)}) collective-permute-start(bf16[64,3,3,1,4,128]{5,0,4,3,2,1:T(8,128)(2,1)S(1)} %pad_maximum_fusion.5), channel_id=1, source_target_pairs={{0,1},{1,2},{2,3},{4,5},{5,6},{6,7},{8,9},{9,10},{10,11},{12,13},{... | collective-permute-start | bytes 1769480 | tf_op jit(solution)/shard_map/ppermute | solution.py:12
where the time goes:
time: 330 us; the launch traced here: 329 us
  blocking collectives  213 us (65%)
  starting transfers between devices  37.7 us (11%)
  other arithmetic  31.6 us (10%)
  waiting for transfers between devices  30.1 us (9%)
  matrix products  9.49 us (3%)
  local copies, waits for them, and re-layouts  6.16 us (2%)
    psum x2, blocking collectives, lower_factor(): total = lax.psum(local_gram, ('tx', 'ty', 'tz'))  213 us
    ppermute x6, waiting for transfers between devices, extended(): lax.ppermute(lax.slice_in_dim(block, 0, width, axis=dim), axis, backward)  23.9 us
    ppermute x6, starting transfers between devices, extended(): lax.ppermute(lax.slice_in_dim(block, block.shape[dim] - width, None, axis...  21.2 us
    ppermute x6, starting transfers between devices, extended(): lax.ppermute(lax.slice_in_dim(block, 0, width, axis=dim), axis, backward)  16.5 us
    another operation x6, other arithmetic, lower_factor(): return jnp.linalg.cholesky(total)  13 us
    another operation x3, other arithmetic, solve_lower(): lax.linalg.triangular_solve(lower, values, left_side=True, lower=True)  10.4 us
  transfers between devices with their start and end apart: 12, of which 10 were waited for; matrix products, arithmetic and copies ran while one was open for 1% of the time, Pallas kernels for 0%

commit v1 on v0

--- a/solution.py
+++ b/solution.py
@@ -40,7 +40,7 @@
     local_gram = jnp.dot(
         mixed, mixed.T, precision=lax.Precision.HIGHEST, preferred_element_type=jnp.float32
     )
-    total = lax.psum(local_gram, ("tx", "ty", "tz"))
+    total = lax.psum(lax.psum(local_gram, ("ty", "tz")), "tx")
     return jnp.linalg.cholesky(total)
 
 

time: 330 us -> 722 us (2.19)
  blocking collectives: 213 us -> 606 us
    psum x2 -> x4, blocking collectives: 213 us -> 606 us  [lower_factor(): total = lax.psum(lax.psum(local_gram, ('ty', 'tz')), 'tx')]
where the time goes in v1:
time: 722 us
  blocking collectives  606 us (84%)
  starting transfers between devices  39.3 us (5%)
  other arithmetic  31.6 us (4%)
  waiting for transfers between devices  28.5 us (4%)
  matrix products  9.49 us (1%)
    psum x4, blocking collectives, lower_factor(): total = lax.psum(lax.psum(local_gram, ('ty', 'tz')), 'tx')  606 us
    ppermute x6, waiting for transfers between devices, extended(): lax.ppermute(lax.slice_in_dim(block, 0, width, axis=dim), axis, backward)  23.2 us
    ppermute x6, starting transfers between devices, extended(): lax.ppermute(lax.slice_in_dim(block, block.shape[dim] - width, None, axis...  19.9 us
    ppermute x6, starting transfers between devices, extended(): lax.ppermute(lax.slice_in_dim(block, 0, width, axis=dim), axis, backward)  19.4 us
  transfers between devices with their start and end apart: 12, of which 10 were waited for; matrix products, arithmetic and copies ran while one was open for 1% of the time, Pallas kernels for 0%

profile of v1, /device:TPU:1, one launch (start us, length us, event | category | flops | bytes accessed | tf_op | source)
XLA Modules:
  0.0 721.7 jit_solution(5620161401243129954)
XLA Ops:
  0.6 0.7 compare_and_fusion.1
  1.3 0.7 compare_select_fusion.1
  2.0 1.1 copy_bitcast_fusion.1
  3.7 8.8 %collective-permute-start.1 = (bf16[64,1,1,1,4,128]{5,0,4,3,2,1:T(8,128)(2,1)S(1)}, bf16[64,1,1,1,4,128]{5,0,4,3,2,1:T(8,128)(2,1)S(1)}, u32[]{:S(2)}, u32[]{:S(2)}) collective-permute-start(bf16[64,1,1,1,4,128]{5,0,4,3,2,1:T(8,128)(2,1)S(1)} %select_bitcast_fusion.1), channel_id=1, source_target_pairs={{64,0},{128,64},{192,128},{256,192},{320,256},{384,320},{448,384},... | collective-permute-start | bytes 196616 | tf_op jit(solution)/shard_map/ppermute | solution.py:15
  12.5 1.9 collective-permute-start
  14.4 0.7 compare_and_fusion
  15.8 1.3 collective-permute-start.3
  17.1 4.0 collective-permute-start.2
  21.1 0.7 compare_select_fusion
  21.9 2.2 collective-permute-done.3
  24.1 0.9 collective-permute-done.2
  25.0 1.3 collective-permute-start.5
  26.3 4.0 collective-permute-start.4
  30.4 2.4 convert_reduce_fusion
  32.8 7.8 %collective-permute-done.5 = bf16[64,3,3,1,4,128]{5,0,4,3,2,1:T(8,128)(2,1)S(1)} collective-permute-done((bf16[64,3,3,1,4,128]{5,0,4,3,2,1:T(8,128)(2,1)S(1)}, bf16[64,3,3,1,4,128]{5,0,4,3,2,1:T(8,128)(2,1)S(1)}, u32[]{:S(2)}, u32[]{:S(2)}) %collective-permute-start.5) | collective-permute-done | bytes 589856 | tf_op jit(solution)/shard_map/ppermute | solution.py:15
  40.6 0.9 collective-permute-done.4
  41.9 2.0 gather_fusion.1
  43.9 3.2 fusion.23
  47.0 0.6 fusion.30
  47.6 230.2 %psum.28 = f32[64,64]{0,1:T(8,128)S(1)} all-reduce(f32[64,64]{0,1:T(8,128)S(1)} %fusion.30), channel_id=1, replica_groups=mesh['tx'=8,'ty'=16,'tz'=4] {'ty','tz'}, use_global_device_ids=true, to_apply=%region_1.4 | all-reduce | flops 4096 | bytes 32768 | tf_op jit(solution)/shard_map/psum | solution.py:43
  277.8 76.7 %psum.29 = f32[64,64]{0,1:T(8,128)S(1)} all-reduce(f32[64,64]{0,1:T(8,128)S(1)} %psum.28), channel_id=1, replica_groups=mesh['tx'=8,'ty'=16,'tz'=4] {'tx'}, use_global_device_ids=true, to_apply=%region_2.5 | all-reduce | flops 4096 | bytes 32768 | tf_op jit(solution)/shard_map/psum | solution.py:43
  354.6 5.8 cholesky.44
  360.5 0.6 compare_reduce_fusion.1
  361.2 0.7 fusion.32
  361.8 4.9 custom-call.6
  366.7 0.7 fusion.29
  368.1 5.4 collective-permute-start.7
  373.5 1.9 collective-permute-start.6
  375.5 1.3 collective-permute-done.6
  376.8 1.3 collective-permute-start.9
  378.1 4.0 collective-permute-start.8
  382.1 3.0 collective-permute-done.9
  385.1 0.9 collective-permute-done.8
  386.1 1.3 collective-permute-start.11
  387.4 4.0 collective-permute-start.10
  391.4 10.2 %collective-permute-done.11 = bf16[64,3,3,1,4,128]{5,0,4,3,2,1:T(8,128)(2,1)S(1)} collective-permute-done((bf16[64,3,3,1,4,128]{5,0,4,3,2,1:T(8,128)(2,1)S(1)}, bf16[64,3,3,1,4,128]{5,0,4,3,2,1:T(8,128)(2,1)S(1)}, u32[]{:S(2)}, u32[]{:S(2)}) %collective-permute-start.11) | collective-permute-done | bytes 589856 | tf_op jit(solution)/shard_map/ppermute | solution.py:15
  401.6 0.9 collective-permute-done.10
  402.9 2.0 gather_fusion.3
  404.9 3.1 fusion.17
  408.0 0.6 fusion.31
  408.6 221.2 %psum.30 = f32[64,64]{0,1:T(8,128)S(1)} all-reduce(f32[64,64]{0,1:T(8,128)S(1)} %fusion.31), channel_id=1, replica_groups=mesh['tx'=8,'ty'=16,'tz'=4] {'ty','tz'}, use_global_device_ids=true, to_apply=%region_5.10 | all-reduce | flops 4096 | bytes 32768 | tf_op jit(solution)/shard_map/psum | solution.py:43
  629.8 77.6 %psum.31 = f32[64,64]{0,1:T(8,128)S(1)} all-reduce(f32[64,64]{0,1:T(8,128)S(1)} %psum.30), channel_id=1, replica_groups=mesh['tx'=8,'ty'=16,'tz'=4] {'tx'}, use_global_device_ids=true, to_apply=%region_6.11 | all-reduce | flops 4096 | bytes 32768 | tf_op jit(solution)/shard_map/psum | solution.py:43
  707.5 5.8 cholesky.55
  713.4 0.6 compare_reduce_fusion
  714.0 0.7 multiply_bitcast_fusion
  714.7 0.7 copy.42
  715.4 4.9 custom-call.7
  720.3 1.4 convolution_multiply_fusion
  (31 shorter events, 3.4 us)
Async XLA Ops:
  3.7 11.5 %collective-permute-start.1 = (bf16[64,1,1,1,4,128]{5,0,4,3,2,1:T(8,128)(2,1)S(1)}, bf16[64,1,1,1,4,128]{5,0,4,3,2,1:T(8,128)(2,1)S(1)}, u32[]{:S(2)}, u32[]{:S(2)}) collective-permute-start(bf16[64,1,1,1,4,128]{5,0,4,3,2,1:T(8,128)(2,1)S(1)} %select_bitcast_fusion.1), channel_id=1, source_target_pairs={{64,0},{128,64},{192,128},{256,192},{320,256},{384,320},{448,384},... | collective-permute-start | bytes 196616 | tf_op jit(solution)/shard_map/ppermute | solution.py:15
  12.5 3.2 collective-permute-start
  15.8 8.3 %collective-permute-start.3 = (bf16[64,3,1,1,4,128]{5,0,4,3,2,1:T(8,128)(2,1)S(1)}, bf16[64,3,1,1,4,128]{5,0,4,3,2,1:T(8,128)(2,1)S(1)}, u32[]{:S(2)}, u32[]{:S(2)}) collective-permute-start(bf16[64,3,1,1,4,128]{5,0,4,3,2,1:T(8,128)(2,1)S(1)} %pad_maximum_fusion.6), channel_id=1, source_target_pairs={{4,0},{8,4},{12,8},{16,12},{20,16},{24,20},{28,24},{32,28},{36,32}... | collective-permute-start | bytes 589832 | tf_op jit(solution)/shard_map/ppermute | solution.py:15
  17.1 7.9 %collective-permute-start.2 = (bf16[64,3,1,1,4,128]{5,0,4,3,2,1:T(8,128)(2,1)S(1)}, bf16[64,3,1,1,4,128]{5,0,4,3,2,1:T(8,128)(2,1)S(1)}, u32[]{:S(2)}, u32[]{:S(2)}) collective-permute-start(bf16[64,3,1,1,4,128]{5,0,4,3,2,1:T(8,128)(2,1)S(1)} %pad_maximum_fusion.6), channel_id=1, source_target_pairs={{0,4},{4,8},{8,12},{12,16},{16,20},{20,24},{24,28},{28,32},{32,36}... | collective-permute-start | bytes 589832 | tf_op jit(solution)/shard_map/ppermute | solution.py:12
  25.0 15.5 %collective-permute-start.5 = (bf16[64,3,3,1,4,128]{5,0,4,3,2,1:T(8,128)(2,1)S(1)}, bf16[64,3,3,1,4,128]{5,0,4,3,2,1:T(8,128)(2,1)S(1)}, u32[]{:S(2)}, u32[]{:S(2)}) collective-permute-start(bf16[64,3,3,1,4,128]{5,0,4,3,2,1:T(8,128)(2,1)S(1)} %pad_maximum_fusion.4), channel_id=1, source_target_pairs={{1,0},{2,1},{3,2},{5,4},{6,5},{7,6},{9,8},{10,9},{11,10},{13,12},{... | collective-permute-start | bytes 1769480 | tf_op jit(solution)/shard_map/ppermute | solution.py:15
  26.3 15.1 %collective-permute-start.4 = (bf16[64,3,3,1,4,128]{5,0,4,3,2,1:T(8,128)(2,1)S(1)}, bf16[64,3,3,1,4,128]{5,0,4,3,2,1:T(8,128)(2,1)S(1)}, u32[]{:S(2)}, u32[]{:S(2)}) collective-permute-start(bf16[64,3,3,1,4,128]{5,0,4,3,2,1:T(8,128)(2,1)S(1)} %pad_maximum_fusion.4), channel_id=1, source_target_pairs={{0,1},{1,2},{2,3},{4,5},{5,6},{6,7},{8,9},{9,10},{10,11},{12,13},{... | collective-permute-start | bytes 1769480 | tf_op jit(solution)/shard_map/ppermute | solution.py:12
  43.9 3.2 copy-start
  368.1 7.4 %collective-permute-start.7 = (bf16[64,1,1,1,4,128]{5,0,4,3,2,1:T(8,128)(2,1)S(1)}, bf16[64,1,1,1,4,128]{5,0,4,3,2,1:T(8,128)(2,1)S(1)}, u32[]{:S(2)}, u32[]{:S(2)}) collective-permute-start(bf16[64,1,1,1,4,128]{5,0,4,3,2,1:T(8,128)(2,1)S(1)} %select_bitcast_fusion), channel_id=1, source_target_pairs={{64,0},{128,64},{192,128},{256,192},{320,256},{384,320},{448,384},... | collective-permute-start | bytes 196616 | tf_op jit(solution)/shard_map/ppermute | solution.py:15
  373.5 3.2 collective-permute-start.6
  376.8 8.3 %collective-permute-start.9 = (bf16[64,3,1,1,4,128]{5,0,4,3,2,1:T(8,128)(2,1)S(1)}, bf16[64,3,1,1,4,128]{5,0,4,3,2,1:T(8,128)(2,1)S(1)}, u32[]{:S(2)}, u32[]{:S(2)}) collective-permute-start(bf16[64,3,1,1,4,128]{5,0,4,3,2,1:T(8,128)(2,1)S(1)} %pad_maximum_fusion.7), channel_id=1, source_target_pairs={{4,0},{8,4},{12,8},{16,12},{20,16},{24,20},{28,24},{32,28},{36,32}... | collective-permute-start | bytes 589832 | tf_op jit(solution)/shard_map/ppermute | solution.py:15
  378.1 7.9 %collective-permute-start.8 = (bf16[64,3,1,1,4,128]{5,0,4,3,2,1:T(8,128)(2,1)S(1)}, bf16[64,3,1,1,4,128]{5,0,4,3,2,1:T(8,128)(2,1)S(1)}, u32[]{:S(2)}, u32[]{:S(2)}) collective-permute-start(bf16[64,3,1,1,4,128]{5,0,4,3,2,1:T(8,128)(2,1)S(1)} %pad_maximum_fusion.7), channel_id=1, source_target_pairs={{0,4},{4,8},{8,12},{12,16},{16,20},{20,24},{24,28},{28,32},{32,36}... | collective-permute-start | bytes 589832 | tf_op jit(solution)/shard_map/ppermute | solution.py:12
  386.1 15.5 %collective-permute-start.11 = (bf16[64,3,3,1,4,128]{5,0,4,3,2,1:T(8,128)(2,1)S(1)}, bf16[64,3,3,1,4,128]{5,0,4,3,2,1:T(8,128)(2,1)S(1)}, u32[]{:S(2)}, u32[]{:S(2)}) collective-permute-start(bf16[64,3,3,1,4,128]{5,0,4,3,2,1:T(8,128)(2,1)S(1)} %pad_maximum_fusion.5), channel_id=1, source_target_pairs={{1,0},{2,1},{3,2},{5,4},{6,5},{7,6},{9,8},{10,9},{11,10},{13,12},{... | collective-permute-start | bytes 1769480 | tf_op jit(solution)/shard_map/ppermute | solution.py:15
  387.4 15.1 %collective-permute-start.10 = (bf16[64,3,3,1,4,128]{5,0,4,3,2,1:T(8,128)(2,1)S(1)}, bf16[64,3,3,1,4,128]{5,0,4,3,2,1:T(8,128)(2,1)S(1)}, u32[]{:S(2)}, u32[]{:S(2)}) collective-permute-start(bf16[64,3,3,1,4,128]{5,0,4,3,2,1:T(8,128)(2,1)S(1)} %pad_maximum_fusion.5), channel_id=1, source_target_pairs={{0,1},{1,2},{2,3},{4,5},{5,6},{6,7},{8,9},{9,10},{10,11},{12,13},{... | collective-permute-start | bytes 1769480 | tf_op jit(solution)/shard_map/ppermute | solution.py:12
